TPU v7x, 256 devices: a whole 4x4x8 slice. The times are simulated.
256 devices in a mesh: mesh: 32 (over x_lo, z, core), mem: 8 (over y, x_hi).
Axes of the slice: x: 4 (x_hi: 2, x_lo: 2; x = x_hi * 2 + x_lo), y: 4, z: 8, core: 2. Of those that a mesh axis runs over, the one named last changes fastest.
Arguments:
- perturbations: bfloat16 [12288, 16384], P('mem', 'mesh')
- node_coord: int32 [16384], P('mesh'), may hold values from 0 to 65535, as said below
- threshold_level: int32 [16384], P('mesh'), may hold values from 0 to 4
Outputs:
- band_cov: float32 [16384, 2048], P(('mesh', 'mem'))
Inputs may be any that keep to these rules, and one draw needn't show every extreme that they name: node_coord[n] lies in 4 n to 4 n + 3; node 0 has 0 and the last node 65535.
All inputs are finite; a program needn't handle non-finite values.
Results may differ from a plain program's by a relative error of at most 0.0003.
Values may be sent and summed in bfloat16 or wider, within the bound.
A program may use at most 64 MiB of HBM per device.

v0:
```python
import jax
import jax.numpy as jnp
from jax import lax
from jax.sharding import PartitionSpec as P

SHIFTS = 3


def shifted(array, axis, by):
    peers = lax.axis_size(axis)
    return lax.ppermute(array, axis, [(i, (i + by) % peers) for i in range(peers)])


def gc_taper(radius):
    near = -0.25 * radius**5 + 0.5 * radius**4 + 0.625 * radius**3 - 5.0 / 3.0 * radius**2 + 1.0
    safe = jnp.maximum(radius, 1.0)
    far = (
        safe**5 / 12.0
        - 0.5 * safe**4
        + 0.625 * safe**3
        + 5.0 / 3.0 * safe**2
        - 5.0 * safe
        + 4.0
        - 2.0 / (3.0 * safe)
    )
    return jnp.where(radius <= 1.0, near, jnp.where(radius <= 2.0, far, 0.0))


def per_device(perturbations, node_coord, threshold_level):
    members_here, width = perturbations.shape
    groups = lax.axis_size("mem")
    period = 4 * width * lax.axis_size("mesh")
    blocks = [(perturbations, node_coord)]
    current = (perturbations, node_coord)
    for step in range(SHIFTS):
        current = shifted((current[0], current[1]), "mesh", -1)
        blocks.append(current)
    owned = width // groups
    first_row = lax.axis_index("mem") * owned
    columns = jnp.concatenate([pair[0] for pair in blocks], axis=1)
    raw = lax.psum_scatter(
        lax.dot_general(
            perturbations, columns, (((0,), (0,)), ((), ())), preferred_element_type=jnp.float32
        ),
        "mem",
        scatter_dimension=0,
        tiled=True,
    )
    cov = raw / jnp.float32(members_here * groups - 1)
    row_coord = lax.dynamic_slice_in_dim(node_coord, first_row, owned, 0)
    row_level = lax.dynamic_slice_in_dim(threshold_level, first_row, owned, 0)
    col_coord = jnp.concatenate([pair[1] for pair in blocks], axis=0)
    gap = jnp.mod(col_coord[None, :] - row_coord[:, None], period)
    dist = jnp.minimum(gap, period - gap).astype(jnp.float32)
    taper = gc_taper(dist / jnp.float32(12 * width))
    level = (0.05 * row_level.astype(jnp.float32))[:, None]
    tapered = taper * cov
    return tapered - jnp.clip(tapered, -level, level)


def solution(mesh):
    in_specs = (P("mem", "mesh"), P("mesh"), P("mesh"))
    out_specs = P(("mesh", "mem"), None)
    return jax.shard_map(
        per_device, mesh=mesh, in_specs=in_specs, out_specs=out_specs, check_vma=False
    )
```

profile of v0, /device:TPU:1, one launch (start us, length us, event | category | flops | bytes accessed | tf_op | source)
XLA Modules:
  0.0 186.2 jit_solution(7283195676210727741)
XLA Ops:
  6.5 0.0 reduce-scatter.4.cloned.1.call-start
  6.5 3.2 %collective-permute-start.3 = (bf16[1536,512]{1,0:T(8,128)(2,1)}, bf16[1536,512]{1,0:T(8,128)(2,1)S(1)}, u32[]{:S(2)}, u32[]{:S(2)}) collective-permute-start(bf16[1536,512]{1,0:T(8,128)(2,1)} %param.3), channel_id=1, source_target_pairs={{0,248},{8,0},{16,8},{24,16},{32,24},{40,32},{48,40},{56,48},{64,5... | collective-permute-start | bytes 4718600 | tf_op jit(solution)/shard_map/ppermute | solution.py:11
  9.7 18.1 %collective-permute-done.3 = bf16[1536,512]{1,0:T(8,128)(2,1)S(1)} collective-permute-done((bf16[1536,512]{1,0:T(8,128)(2,1)}, bf16[1536,512]{1,0:T(8,128)(2,1)S(1)}, u32[]{:S(2)}, u32[]{:S(2)}) %collective-permute-start.3) | collective-permute-done | bytes 1572896 | tf_op jit(solution)/shard_map/ppermute | solution.py:11
  27.9 4.6 %collective-permute-start.4 = (bf16[1536,512]{1,0:T(8,128)(2,1)S(1)}, bf16[1536,512]{1,0:T(8,128)(2,1)S(1)}, u32[]{:S(2)}, u32[]{:S(2)}) collective-permute-start(bf16[1536,512]{1,0:T(8,128)(2,1)S(1)} %collective-permute-done.3), channel_id=1, source_target_pairs={{0,248},{8,0},{16,8},{24,16},{32,24},{40,32},{48,40},{56,48},{64,5... | collective-permute-start | bytes 4718600 | tf_op jit(solution)/shard_map/ppermute | solution.py:11
  32.5 15.2 %collective-permute-done.4 = bf16[1536,512]{1,0:T(8,128)(2,1)S(1)} collective-permute-done((bf16[1536,512]{1,0:T(8,128)(2,1)S(1)}, bf16[1536,512]{1,0:T(8,128)(2,1)S(1)}, u32[]{:S(2)}, u32[]{:S(2)}) %collective-permute-start.4) | collective-permute-done | bytes 1572896 | tf_op jit(solution)/shard_map/ppermute | solution.py:11
  47.7 6.6 %collective-permute-start.5 = (bf16[1536,512]{1,0:T(8,128)(2,1)S(1)}, bf16[1536,512]{1,0:T(8,128)(2,1)S(1)}, u32[]{:S(2)}, u32[]{:S(2)}) collective-permute-start(bf16[1536,512]{1,0:T(8,128)(2,1)S(1)} %collective-permute-done.4), channel_id=1, source_target_pairs={{0,248},{8,0},{16,8},{24,16},{32,24},{40,32},{48,40},{56,48},{64,5... | collective-permute-start | bytes 4718600 | tf_op jit(solution)/shard_map/ppermute | solution.py:11
  54.4 13.2 %collective-permute-done.5 = bf16[1536,512]{1,0:T(8,128)(2,1)S(1)} collective-permute-done((bf16[1536,512]{1,0:T(8,128)(2,1)S(1)}, bf16[1536,512]{1,0:T(8,128)(2,1)S(1)}, u32[]{:S(2)}, u32[]{:S(2)}) %collective-permute-start.5) | collective-permute-done | bytes 1572896 | tf_op jit(solution)/shard_map/ppermute | solution.py:11
  67.5 7.7 %fusion.8 = f32[512,2048]{0,1:T(8,128)} fusion(bf16[1536,512]{1,0:T(8,128)(2,1)} %param.3, bf16[1536,512]{1,0:T(8,128)(2,1)S(1)} %collective-permute-done.5, bf16[1536,512]{1,0:T(8,128)(2,1)S(1)} %collective-permute-done.4, bf16[1536,512]{1,0:T(8,128)(2,1)S(1)} %collective-permute-done.3), kind=kOutput, calls=%fused_computation.8 | convolution fusion | flops 3246391296 | bytes 10485760 | tf_op jit(solution)/shard_map/dot_general | solution.py:42
  75.2 5.4 %copy.7 = f32[512,2048]{1,0:T(8,128)} copy(f32[512,2048]{0,1:T(8,128)} %fusion.8) | data formatting | bytes 8388608
  80.6 0.0 copy-start
  80.6 0.0 reduce-scatter.4.cloned.1.call-update
  80.7 0.7 copy-done
  81.3 8.7 %collective-permute-start = (s32[512]{0:T(512)S(1)}, s32[512]{0:T(512)S(1)}, u32[]{:S(2)}, u32[]{:S(2)}) collective-permute-start(s32[512]{0:T(512)S(1)} %copy-done), channel_id=1, source_target_pairs={{0,248},{8,0},{16,8},{24,16},{32,24},{40,32},{48,40},{56,48},{64,5... | collective-permute-start | bytes 6152 | tf_op jit(solution)/shard_map/ppermute | solution.py:11
  90.0 0.8 collective-permute-done
  90.9 4.5 %collective-permute-start.1 = (s32[512]{0:T(512)S(1)}, s32[512]{0:T(512)S(1)}, u32[]{:S(2)}, u32[]{:S(2)}) collective-permute-start(s32[512]{0:T(512)S(1)} %collective-permute-done), channel_id=1, source_target_pairs={{0,248},{8,0},{16,8},{24,16},{32,24},{40,32},{48,40},{56,48},{64,5... | collective-permute-start | bytes 6152 | tf_op jit(solution)/shard_map/ppermute | solution.py:11
  95.4 0.8 collective-permute-done.1
  96.2 4.3 %collective-permute-start.2 = (s32[512]{0:T(512)S(1)}, s32[512]{0:T(512)S(1)}, u32[]{:S(2)}, u32[]{:S(2)}) collective-permute-start(s32[512]{0:T(512)S(1)} %collective-permute-done.1), channel_id=1, source_target_pairs={{0,248},{8,0},{16,8},{24,16},{32,24},{40,32},{48,40},{56,48},{64,5... | collective-permute-start | bytes 6152 | tf_op jit(solution)/shard_map/ppermute | solution.py:11
  100.5 0.8 fusion.37
  101.3 0.1 dynamic_slice.6
  101.4 0.0 collective-permute-done.2
  101.4 75.2 %reduce-scatter.4.cloned.1.call-done = f32[64,2048]{1,0:T(8,128)} async-done(((f32[512,2048]{1,0:T(8,128)}), f32[64,2048]{1,0:T(8,128)}) %reduce-scatter.4.cloned.1.call-update) | async-done | bytes 524304 | tf_op jit(solution)/shard_map/reduce_scatter | solution.py:41
  176.5 2.9 %minimum_subtract_fusion = f32[64,2048]{1,0:T(8,128)} fusion(f32[64,2048]{1,0:T(8,128)} %reduce-scatter.4.cloned.1.call-done, f32[64]{0:T(128)S(1)} %get-tuple-element.5, f32[64]{0:T(128)S(1)} %get-tuple-element.6, s32[64]{0:T(128)S(1)} %dynamic_slice.6, s32[2048]{0:T(1024)S(1)} %pad_add_fusion), kind=kLoop, calls=%fused_computation.48 | loop fusion | flops 7208960 | bytes 1057536 | tf_op jit(solution)/shard_map/sub | solution.py:58
  (1 shorter events, 0.0 us)
Async XLA Ops:
  6.5 170.0 %reduce-scatter.4.cloned.1.call-start = ((), (), s32[]{:S(2)}) async-start(), calls=%async_computation.1 | async-start | bytes 4718592 | tf_op jit(solution)/shard_map/reduce_scatter | solution.py:41
  6.5 21.3 %collective-permute-start.3 = (bf16[1536,512]{1,0:T(8,128)(2,1)}, bf16[1536,512]{1,0:T(8,128)(2,1)S(1)}, u32[]{:S(2)}, u32[]{:S(2)}) collective-permute-start(bf16[1536,512]{1,0:T(8,128)(2,1)} %param.3), channel_id=1, source_target_pairs={{0,248},{8,0},{16,8},{24,16},{32,24},{40,32},{48,40},{56,48},{64,5... | collective-permute-start | bytes 4718600 | tf_op jit(solution)/shard_map/ppermute | solution.py:11
  27.9 19.8 %collective-permute-start.4 = (bf16[1536,512]{1,0:T(8,128)(2,1)S(1)}, bf16[1536,512]{1,0:T(8,128)(2,1)S(1)}, u32[]{:S(2)}, u32[]{:S(2)}) collective-permute-start(bf16[1536,512]{1,0:T(8,128)(2,1)S(1)} %collective-permute-done.3), channel_id=1, source_target_pairs={{0,248},{8,0},{16,8},{24,16},{32,24},{40,32},{48,40},{56,48},{64,5... | collective-permute-start | bytes 4718600 | tf_op jit(solution)/shard_map/ppermute | solution.py:11
  47.7 19.8 %collective-permute-start.5 = (bf16[1536,512]{1,0:T(8,128)(2,1)S(1)}, bf16[1536,512]{1,0:T(8,128)(2,1)S(1)}, u32[]{:S(2)}, u32[]{:S(2)}) collective-permute-start(bf16[1536,512]{1,0:T(8,128)(2,1)S(1)} %collective-permute-done.4), channel_id=1, source_target_pairs={{0,248},{8,0},{16,8},{24,16},{32,24},{40,32},{48,40},{56,48},{64,5... | collective-permute-start | bytes 4718600 | tf_op jit(solution)/shard_map/ppermute | solution.py:11
  80.6 0.7 copy-start
  81.3 9.5 %collective-permute-start = (s32[512]{0:T(512)S(1)}, s32[512]{0:T(512)S(1)}, u32[]{:S(2)}, u32[]{:S(2)}) collective-permute-start(s32[512]{0:T(512)S(1)} %copy-done), channel_id=1, source_target_pairs={{0,248},{8,0},{16,8},{24,16},{32,24},{40,32},{48,40},{56,48},{64,5... | collective-permute-start | bytes 6152 | tf_op jit(solution)/shard_map/ppermute | solution.py:11
  90.9 5.4 %collective-permute-start.1 = (s32[512]{0:T(512)S(1)}, s32[512]{0:T(512)S(1)}, u32[]{:S(2)}, u32[]{:S(2)}) collective-permute-start(s32[512]{0:T(512)S(1)} %collective-permute-done), channel_id=1, source_target_pairs={{0,248},{8,0},{16,8},{24,16},{32,24},{40,32},{48,40},{56,48},{64,5... | collective-permute-start | bytes 6152 | tf_op jit(solution)/shard_map/ppermute | solution.py:11
  96.2 5.1 %collective-permute-start.2 = (s32[512]{0:T(512)S(1)}, s32[512]{0:T(512)S(1)}, u32[]{:S(2)}, u32[]{:S(2)}) collective-permute-start(s32[512]{0:T(512)S(1)} %collective-permute-done.1), channel_id=1, source_target_pairs={{0,248},{8,0},{16,8},{24,16},{32,24},{40,32},{48,40},{56,48},{64,5... | collective-permute-start | bytes 6152 | tf_op jit(solution)/shard_map/ppermute | solution.py:11
Sparse Core Ops, SparseCore 0:
  80.8 95.6 reduce-scatter.3
where the time goes:
time: 187 us; the launch traced here: 186 us
  waiting for transfers between devices  123 us (66%)
  starting transfers between devices  32.1 us (17%)
  between operations  13.4 us (7%)
  matrix products  7.68 us (4%)
  local copies, waits for them, and re-layouts  6.14 us (3%)
  other arithmetic  3.64 us (2%)
    reduce_scatter x1, waiting for transfers between devices, per_device(): lax.psum_scatter(lax.dot_general(perturbations, columns, (((0,), (0,)), (...  75.2 us
    ppermute x6, waiting for transfers between devices, shifted(): lax.ppermute(array, axis, [(i, (i + by) % peers) for i in range(peers)])  48.2 us
    ppermute x6, starting transfers between devices, shifted(): lax.ppermute(array, axis, [(i, (i + by) % peers) for i in range(peers)])  32 us
    dot_general x1, matrix products, per_device(): lax.dot_general(perturbations, columns, (((0,), (0,)), ((), ())), preferr...  7.68 us
    unnamed x3, local copies, waits for them, and re-layouts  6.07 us
  transfers between devices with their start and end apart: 7, of which 6 were waited for; matrix products, arithmetic and copies ran while one was open for 0% of the time, Pallas kernels for 0%

commit v1 on v0

v1 whole, which is shorter than its diff:
```python
import functools

import jax
import jax.numpy as jnp
from jax import lax
from jax.experimental import pallas as pl
from jax.experimental.pallas import tpu as pltpu
from jax.sharding import PartitionSpec as P

MESH = pl.DeviceIdType.MESH
LANES = 128
STEPS = 32000.0
F32 = jnp.float32


def gc_taper(radius):
    r2 = radius * radius
    r3 = r2 * radius
    near = r3 * (0.625 + radius * (0.5 - 0.25 * radius)) - (5.0 / 3.0) * r2 + 1.0
    safe = jnp.maximum(radius, 1.0)
    s2 = safe * safe
    s3 = s2 * safe
    far = s3 * (0.625 + safe * (safe / 12.0 - 0.5)) + (5.0 / 3.0) * s2 - 5.0 * safe + 4.0 - 2.0 / (3.0 * safe)
    return jnp.where(radius <= 1.0, near, jnp.where(radius <= 2.0, far, 0.0))


def encode(blocks, store):
    top = functools.reduce(jnp.maximum, [jnp.max(jnp.abs(b), axis=0, keepdims=True) for b in blocks])
    power = jnp.ceil(jnp.log2(jnp.maximum(top, 1.2e-38)))
    half = jnp.floor(0.5 * power)
    one, two = jnp.exp2(-half), jnp.exp2(half - power) * STEPS
    at = 0
    for b in blocks:
        rows = b.shape[0]
        store(at, rows, jnp.round((b * one) * two).astype(jnp.int32).astype(jnp.int16))
        at += rows
    store(at, 16, jnp.broadcast_to(power, (16, LANES)).astype(jnp.int32).astype(jnp.int16))


def scale_of(ref, rows):
    power = ref[pl.ds(rows, 16), :].astype(jnp.int32).astype(F32)[0:1]
    half = jnp.floor(0.5 * power)
    return jnp.exp2(half), jnp.exp2(power - half) / STEPS


def decode(ref, at, rows, scale):
    return (ref[pl.ds(at, rows), :].astype(jnp.int32).astype(F32) * scale[0]) * scale[1]


def kernel(
    members, parts, period, reach,
    x_ref, coord_ref, level_ref, out_ref,
    held, turned, coords, rowv, weight, own_e, own_l, keep_e, keep_l, split,
    ysend_e, yrecv_e, ysend_l, yrecv_l, fsend_e, frecv_e, fsend_l, frecv_l,
    own_sem, zs, zr, bs, br, us, ur, cs, cr, yse, yre, ysl, yrl, fse, fre, fsl, frl,
):
    p, m = lax.axis_index("mesh"), lax.axis_index("mem")
    core, y, h = lax.rem(p, 2), m // 2, lax.rem(m, 2)
    far = m + 1 - 2 * h
    sib = p + 1 - 2 * core

    def at(shift):
        return lax.rem(p + shift + parts, parts)

    def ring(d):
        return (p, lax.rem(m + 2 * d, 8))

    barrier = pltpu.get_barrier_semaphore()
    peers = [(at(s), m) for s in (-3, -2, -1, 1, 2, 3)] + [ring(d) for d in (1, 2, 3)]
    peers += [(p, far), (at(1), far), (at(-1), far)]
    for peer in peers:
        pl.semaphore_signal(barrier, inc=1, device_id=peer, device_id_type=MESH)
    pl.semaphore_wait(barrier, len(peers))

    def send(src, dst, ssem, rsem, to):
        return pltpu.make_async_remote_copy(
            src_ref=src, dst_ref=dst, send_sem=ssem, recv_sem=rsem, device_id=to, device_id_type=MESH
        )

    def columns(j):
        return pl.ds(pl.multiple_of(j * LANES, LANES), LANES)

    def down(j):
        c = pl.ds(j * LANES, LANES)
        return send(x_ref.at[:, c], held.at[2, :, c], zs.at[j], zr.at[j], (at(-2), m))

    beside = send(x_ref, held.at[1], bs, br, (sib, m))
    up = send(x_ref, held.at[3], us, ur, (at(1), m))
    notes = [send(coord_ref, coords.at[k], cs.at[k], cr.at[k], (at(-1 - k), m)) for k in range(3)]
    beside.start()
    down(0).start()

    @pl.when(core == 1)
    def _():
        up.start()

    for j in range(1, 4):
        down(j).start()
    for note in notes:
        note.start()
    mine = pltpu.make_async_copy(x_ref, held.at[0], own_sem)
    mine.start()
    mine.wait()

    def turn(slot, to):
        def body(q, carry):
            turned[q, to] = held[slot, :, columns(q)].T
            return carry

        lax.fori_loop(0, 4, body, 0)

    turn(0, 0)

    def e_blocks(row):
        full = jnp.dot(turned[row, 0], held[0], preferred_element_type=F32)
        return [full[:, k * LANES : (k + 1) * LANES] for k in range(4)]

    def y_e(d):
        return send(ysend_e.at[d - 1], yrecv_e.at[d - 1], yse.at[d - 1], yre.at[d - 1], ring(d))

    for d in (2, 1, 3):

        def put(a, n, v, d=d):
            ysend_e[d - 1, pl.ds(a, n), :] = v

        encode(e_blocks(lax.rem(y + d, 4)), put)
        y_e(d).start()
    for k, b in enumerate(e_blocks(y)):
        own_e[k] = b

    def as_rows(ref):
        line = ref[0:1, columns(y)].astype(F32)
        return jnp.broadcast_to(line, (LANES, LANES)).T

    for k, ref in enumerate((coord_ref, level_ref)):
        v = as_rows(ref)
        rowv[k, 0] = v[0:64]
        rowv[k, 1] = v[64:128]
    row = rowv[0, h]
    limit = 0.05 * rowv[1, h]
    for note in notes:
        note.wait_recv()
    for s in range(4):
        for j in range(4):
            c = pl.ds(j * LANES, LANES)
            col = (coord_ref[0:1, c] if s == 0 else coords[s - 1, 0:1, c]).astype(F32)
            gap = col - row
            gap = jnp.where(gap < 0.0, gap + period, gap)
            dist = jnp.minimum(gap, period - gap)
            weight[s, j] = gc_taper(dist / reach) * (1.0 / (members - 1.0))

    def finish(value, s, j):
        c = weight[s, j] * value
        out_ref[:, pl.ds(pl.multiple_of((s * 4 + j) * LANES, LANES), LANES)] = c - jnp.clip(c, -limit, limit)

    beside.wait_recv()
    turn(1, 1)

    f_e = send(fsend_e, frecv_e, fse, fre, (p, far))
    for d in (1, 2, 3):
        y_e(d).wait_recv()
    scales = [scale_of(yrecv_e.at[d], 512) for d in range(3)]
    theirs = []
    for k in range(4):
        total = own_e[k]
        for d in range(3):
            total = total + decode(yrecv_e.at[d], k * LANES, LANES, scales[d])
        split[0, 0] = total[0:64]
        split[0, 1] = total[64:128]
        keep_e[k] = split[0, h]
        theirs.append(split[0, 1 - h])

    def put_e(a, n, v):
        fsend_e[pl.ds(a, n), :] = v

    encode(theirs, put_e)
    f_e.start()

    @pl.when(core == 0)
    def _():
        up.wait_recv()
        turn(3, 2)

    f_e.wait_recv()
    scale = scale_of(frecv_e, 256)
    for k in range(4):
        finish(keep_e[k] + decode(frecv_e, k * 64, 64, scale), 0, k)

    lhs2, rhs2 = 1 + (1 - core), 2 * (1 - core)

    def l_blocks(row, j):
        c = pl.ds(j * LANES, LANES)
        pair = turned[row, 0:2].reshape(2 * LANES, members // 8)
        both = jnp.dot(pair, held[2, :, c], preferred_element_type=F32)
        third = jnp.dot(turned[row, lhs2], held[rhs2, :, c], preferred_element_type=F32)
        return [both[0:LANES], both[LANES:], third]

    def y_l(j, d):
        return send(ysend_l.at[j, d - 1], yrecv_l.at[j, d - 1], ysl.at[j, d - 1], yrl.at[j, d - 1], ring(d))

    def first(j):
        down(j).wait_recv()
        for d in (2, 1, 3):

            def put(a, n, v, d=d):
                ysend_l[j, d - 1, pl.ds(a, n), :] = v

            encode(l_blocks(lax.rem(y + d, 4), j), put)
            y_l(j, d).start()
        for k, b in enumerate(l_blocks(y, j)):
            own_l[j, k] = b

    goals = [(p, far), (sib, m), (sib, far), (at(-1), m), (at(-1), far)]

    def f_l(j, i):
        return send(fsend_l.at[j, i], frecv_l.at[j, i], fsl.at[j, i], frl.at[j, i], goals[i])

    def second(j):
        for d in (1, 2, 3):
            y_l(j, d).wait_recv()
        scales = [scale_of(yrecv_l.at[j, d], 384) for d in range(3)]
        for k in range(3):
            total = own_l[j, k]
            for d in range(3):
                total = total + decode(yrecv_l.at[j, d], k * LANES, LANES, scales[d])
            split[k, 0] = total[0:64]
            split[k, 1] = total[64:128]
        keep_l[j] = split[0, h]
        for i, (k, half) in enumerate([(0, 1 - h), (1, h), (1, 1 - h), (2, h), (2, 1 - h)]):

            def put(a, n, v, i=i):
                fsend_l[j, i, pl.ds(a, n), :] = v

            encode([split[k, half]], put)
            f_l(j, i).start()

    def third(j):
        for i in range(5):
            f_l(j, i).wait_recv()
        got = [decode(frecv_l.at[j, i], 0, 64, scale_of(frecv_l.at[j, i], 64)) for i in range(5)]
        finish(keep_l[j] + got[0], 2, j)
        finish(got[1] + got[2], 3 - 2 * core, j)
        finish(got[3] + got[4], 1 + 2 * core, j)

    first(0)
    first(1)
    second(0)
    first(2)
    second(1)
    third(0)
    first(3)
    second(2)
    third(1)
    second(3)
    third(2)
    third(3)

    beside.wait_send()

    @pl.when(core == 1)
    def _():
        up.wait_send()

    for note in notes:
        note.wait_send()
    f_e.wait_send()
    for d in (1, 2, 3):
        y_e(d).wait_send()
    for j in range(4):
        down(j).wait_send()
        for d in (1, 2, 3):
            y_l(j, d).wait_send()
        for i in range(5):
            f_l(j, i).wait_send()


def solution(mesh):
    parts, groups = mesh.shape["mesh"], mesh.shape["mem"]

    def per_device(x, coord, level):
        rows, width = x.shape
        owned = width // groups
        dma, vmem, i16 = pltpu.SemaphoreType.DMA, pltpu.VMEM, jnp.int16
        body = functools.partial(kernel, rows * groups, parts, 4.0 * width * parts, 12.0 * width)
        any_space, in_vmem = pl.BlockSpec(memory_space=pl.ANY), pl.BlockSpec(memory_space=pltpu.VMEM)
        return pl.pallas_call(
            body,
            out_shape=jax.ShapeDtypeStruct((owned, 4 * width), F32),
            in_specs=[any_space, in_vmem, in_vmem],
            out_specs=in_vmem,
            scratch_shapes=[
                vmem((4, rows, width), jnp.bfloat16),
                vmem((4, 3, LANES, rows), jnp.bfloat16),
                vmem((3, 1, width), jnp.int32),
                vmem((2, 2, 64, LANES), F32),
                vmem((4, 4, 64, LANES), F32),
                vmem((4, LANES, LANES), F32),
                vmem((4, 3, LANES, LANES), F32),
                vmem((4, 64, LANES), F32),
                vmem((4, 64, LANES), F32),
                vmem((3, 2, 64, LANES), F32),
                vmem((3, 528, LANES), i16),
                vmem((3, 528, LANES), i16),
                vmem((4, 3, 400, LANES), i16),
                vmem((4, 3, 400, LANES), i16),
                vmem((272, LANES), i16),
                vmem((272, LANES), i16),
                vmem((4, 5, 80, LANES), i16),
                vmem((4, 5, 80, LANES), i16),
                dma, dma((4,)), dma((4,)), dma, dma, dma, dma, dma((3,)), dma((3,)),
                dma((3,)), dma((3,)), dma((4, 3)), dma((4, 3)), dma, dma, dma((4, 5)), dma((4, 5)),
            ],
            compiler_params=pltpu.CompilerParams(
                collective_id=0, has_side_effects=True, vmem_limit_bytes=48 << 20
            ),
        )(x, coord.reshape(1, width), level.reshape(1, width))

    in_specs = (P("mem", "mesh"), P("mesh"), P("mesh"))
    out_specs = P(("mesh", "mem"), None)
    return jax.shard_map(per_device, mesh=mesh, in_specs=in_specs, out_specs=out_specs, check_vma=False)
```

time: 187 us -> 79.1 us (0.42)
  waiting for transfers between devices: 123 us -> 0 us
  Pallas kernels: 0 us -> 74.4 us
  starting transfers between devices: 32.1 us -> 0 us
  between operations: 13.4 us -> 0.01 us
  matrix products: 7.68 us -> 0 us
  other arithmetic: 3.64 us -> 0 us
  local copies, waits for them, and re-layouts: 6.14 us -> 3.57 us
    reduce_scatter x1 -> x0, waiting for transfers between devices: 75.2 us -> none  [per_device(): lax.psum_scatter(lax.dot_general(perturbations, columns, (((0,), (0,)), (...]
    pallas_call x0 -> x1, Pallas kernels: none -> 74.4 us  [per_device(): pl.pallas_call(body, out_shape=jax.ShapeDtypeStruct((owned, 4 * width), F...]
    ppermute x6 -> x0, waiting for transfers between devices: 48.2 us -> none  [shifted(): lax.ppermute(array, axis, [(i, (i + by) % peers) for i in range(peers)])]
    ppermute x6 -> x0, starting transfers between devices: 32 us -> none  [shifted(): lax.ppermute(array, axis, [(i, (i + by) % peers) for i in range(peers)])]
    dot_general x1 -> x0, matrix products: 7.68 us -> none  [per_device(): lax.dot_general(perturbations, columns, (((0,), (0,)), ((), ())), preferr...]
    sub x1 -> x0, other arithmetic: 2.87 us -> none  [per_device(): return tapered - jnp.clip(tapered, -level, level)]
    unnamed x3 -> x7, local copies, waits for them, and re-layouts: 6.07 us -> 3.57 us
  transfers between devices with their start and end apart: 7 -> 0, of which waited for: 6 -> 0; matrix products, arithmetic and copies ran while one was open for 0% -> 0% of each run, Pallas kernels for 0% -> 0%
where the time goes in v1:
time: 79.1 us; the launch traced here: 78 us
  Pallas kernels  74.4 us (94%)
  local copies, waits for them, and re-layouts  3.57 us (5%)
    pallas_call x1, Pallas kernels, per_device(): pl.pallas_call(body, out_shape=jax.ShapeDtypeStruct((owned, 4 * width), F...  74.4 us
    unnamed x7, local copies, waits for them, and re-layouts  3.57 us

profile of v1, /device:TPU:1, one launch (start us, length us, event | category | flops | bytes accessed | tf_op | source)
XLA Modules:
  0.0 78.0 jit_solution(11532537706289572908)
XLA Ops:
  0.0 0.0 copy-start
  0.0 1.4 %copy-done = bf16[1536,512]{1,0:T(8,128)(2,1)S(1)} copy-done((bf16[1536,512]{1,0:T(8,128)(2,1)S(1)}, bf16[1536,512]{1,0:T(8,128)(2,1)}, u32[]{:S(2)}) %copy-start) | copy-done | bytes 1572888
  1.4 0.0 copy-start.1
  1.4 0.7 copy-done.1
  2.1 0.0 copy-start.2
  2.1 0.7 copy-done.2
  2.8 74.4 %shard_map.37 = f32[64,2048]{1,0:T(8,128)S(1)} custom-call(bf16[1536,512]{1,0:T(8,128)(2,1)S(1)} %copy-done, s32[1,512]{1,0:T(1,128)S(1)} %bitcast.2, s32[1,512]{1,0:T(1,128)S(1)} %bitcast.3), custom_call_target="tpu_custom_call" | custom-call | tf_op jit(solution)/shard_map/pallas_call | solution.py:286
  77.2 0.8 %copy.5 = f32[64,2048]{1,0:T(8,128)} copy(f32[64,2048]{1,0:T(8,128)S(1)} %shard_map.37) | data formatting | bytes 1048576
Async XLA Ops:
  0.0 1.4 %copy-start = (bf16[1536,512]{1,0:T(8,128)(2,1)S(1)}, bf16[1536,512]{1,0:T(8,128)(2,1)}, u32[]{:S(2)}) copy-start(bf16[1536,512]{1,0:T(8,128)(2,1)} %x_ref.1) | copy-start | bytes 4718596
  1.4 0.7 copy-start.1
  2.1 0.7 copy-start.2

commit v2 on v1

--- a/solution.py
+++ b/solution.py
@@ -49,10 +49,10 @@
 
 def kernel(
     members, parts, period, reach,
-    x_ref, coord_ref, level_ref, out_ref,
-    held, turned, coords, rowv, weight, own_e, own_l, keep_e, keep_l, split,
+    x_ref, coord_hbm, level_hbm, out_ref,
+    coord_ref, level_ref, held, turned, coords, rowv, weight, own_e, own_l, keep_e, keep_l, split,
     ysend_e, yrecv_e, ysend_l, yrecv_l, fsend_e, frecv_e, fsend_l, frecv_l,
-    own_sem, zs, zr, bs, br, us, ur, cs, cr, yse, yre, ysl, yrl, fse, fre, fsl, frl,
+    own_sem, note_sem, zs, zr, bs, br, us, ur, cs, cr, yse, yre, ysl, yrl, fse, fre, fsl, frl,
 ):
     p, m = lax.axis_index("mesh"), lax.axis_index("mem")
     core, y, h = lax.rem(p, 2), m // 2, lax.rem(m, 2)
@@ -64,6 +64,14 @@
 
     def ring(d):
         return (p, lax.rem(m + 2 * d, 8))
+
+    mine = [
+        pltpu.make_async_copy(x_ref, held.at[0], own_sem),
+        pltpu.make_async_copy(coord_hbm, coord_ref, note_sem.at[0]),
+        pltpu.make_async_copy(level_hbm, level_ref, note_sem.at[1]),
+    ]
+    for copy in mine:
+        copy.start()
 
     barrier = pltpu.get_barrier_semaphore()
     peers = [(at(s), m) for s in (-3, -2, -1, 1, 2, 3)] + [ring(d) for d in (1, 2, 3)]
@@ -77,30 +85,42 @@
             src_ref=src, dst_ref=dst, send_sem=ssem, recv_sem=rsem, device_id=to, device_id_type=MESH
         )
 
+    piece, started = members // 32, [0, 0]
+
     def columns(j):
         return pl.ds(pl.multiple_of(j * LANES, LANES), LANES)
 
-    def down(j):
-        c = pl.ds(j * LANES, LANES)
-        return send(x_ref.at[:, c], held.at[2, :, c], zs.at[j], zr.at[j], (at(-2), m))
+    def down(i):
+        c, r = pl.ds(i // 4 * LANES, LANES), pl.ds(i % 4 * piece, piece)
+        return send(x_ref.at[r, c], held.at[2, r, c], zs.at[i], zr.at[i], (at(-2), m))
+
+    def pump(*counts):
+        for who, count in enumerate(counts):
+            if count:
+                todo = range(started[who], started[who] + count)
+                started[who] += count
+
+                @pl.when(core == who)
+                def _(todo=todo):
+                    for i in todo:
+                        if i >= 4:
+                            down(i - 4).wait_send()
+                        down(i).start()
 
     beside = send(x_ref, held.at[1], bs, br, (sib, m))
     up = send(x_ref, held.at[3], us, ur, (at(1), m))
-    notes = [send(coord_ref, coords.at[k], cs.at[k], cr.at[k], (at(-1 - k), m)) for k in range(3)]
+    notes = [send(coord_hbm, coords.at[k], cs.at[k], cr.at[k], (at(-1 - k), m)) for k in range(3)]
+    for note in notes:
+        note.start()
     beside.start()
-    down(0).start()
 
     @pl.when(core == 1)
     def _():
         up.start()
 
-    for j in range(1, 4):
-        down(j).start()
-    for note in notes:
-        note.start()
-    mine = pltpu.make_async_copy(x_ref, held.at[0], own_sem)
-    mine.start()
-    mine.wait()
+    pump(4, 0)
+    for copy in mine:
+        copy.wait()
 
     def turn(slot, to):
         def body(q, carry):
@@ -127,6 +147,8 @@
         y_e(d).start()
     for k, b in enumerate(e_blocks(y)):
         own_e[k] = b
+
+    pump(3, 3)
 
     def as_rows(ref):
         line = ref[0:1, columns(y)].astype(F32)
@@ -155,6 +177,7 @@
 
     beside.wait_recv()
     turn(1, 1)
+    pump(3, 3)
 
     f_e = send(fsend_e, frecv_e, fse, fre, (p, far))
     for d in (1, 2, 3):
@@ -175,16 +198,19 @@
 
     encode(theirs, put_e)
     f_e.start()
+    for _ in range(4):
+        pump(1, 1)
 
     @pl.when(core == 0)
     def _():
         up.wait_recv()
         turn(3, 2)
 
-    f_e.wait_recv()
-    scale = scale_of(frecv_e, 256)
-    for k in range(4):
-        finish(keep_e[k] + decode(frecv_e, k * 64, 64, scale), 0, k)
+    def third_e():
+        f_e.wait_recv()
+        scale = scale_of(frecv_e, 256)
+        for k in range(4):
+            finish(keep_e[k] + decode(frecv_e, k * 64, 64, scale), 0, k)
 
     lhs2, rhs2 = 1 + (1 - core), 2 * (1 - core)
 
@@ -199,7 +225,8 @@
         return send(ysend_l.at[j, d - 1], yrecv_l.at[j, d - 1], ysl.at[j, d - 1], yrl.at[j, d - 1], ring(d))
 
     def first(j):
-        down(j).wait_recv()
+        for i in range(4):
+            down(4 * j + i).wait_recv()
         for d in (2, 1, 3):
 
             def put(a, n, v, d=d):
@@ -243,17 +270,23 @@
         finish(got[3] + got[4], 1 + 2 * core, j)
 
     first(0)
+    pump(1, 1)
     first(1)
+    pump(1, 1)
     second(0)
+    pump(0, 2)
+    pump(0, 2)
     first(2)
     second(1)
+    first(3)
+    third_e()
     third(0)
-    first(3)
     second(2)
     third(1)
     second(3)
     third(2)
     third(3)
+    assert started == [16, 16]
 
     beside.wait_send()
 
@@ -266,8 +299,9 @@
     f_e.wait_send()
     for d in (1, 2, 3):
         y_e(d).wait_send()
+    for i in range(12, 16):
+        down(i).wait_send()
     for j in range(4):
-        down(j).wait_send()
         for d in (1, 2, 3):
             y_l(j, d).wait_send()
         for i in range(5):
@@ -282,13 +316,15 @@
         owned = width // groups
         dma, vmem, i16 = pltpu.SemaphoreType.DMA, pltpu.VMEM, jnp.int16
         body = functools.partial(kernel, rows * groups, parts, 4.0 * width * parts, 12.0 * width)
-        any_space, in_vmem = pl.BlockSpec(memory_space=pl.ANY), pl.BlockSpec(memory_space=pltpu.VMEM)
+        in_hbm = pl.BlockSpec(memory_space=pltpu.HBM)
         return pl.pallas_call(
             body,
             out_shape=jax.ShapeDtypeStruct((owned, 4 * width), F32),
-            in_specs=[any_space, in_vmem, in_vmem],
-            out_specs=in_vmem,
+            in_specs=[in_hbm] * 3,
+            out_specs=pl.BlockSpec(memory_space=pltpu.VMEM),
             scratch_shapes=[
+                vmem((1, width), jnp.int32),
+                vmem((1, width), jnp.int32),
                 vmem((4, rows, width), jnp.bfloat16),
                 vmem((4, 3, LANES, rows), jnp.bfloat16),
                 vmem((3, 1, width), jnp.int32),
@@ -307,11 +343,11 @@
                 vmem((272, LANES), i16),
                 vmem((4, 5, 80, LANES), i16),
                 vmem((4, 5, 80, LANES), i16),
-                dma, dma((4,)), dma((4,)), dma, dma, dma, dma, dma((3,)), dma((3,)),
+                dma, dma((2,)), dma((16,)), dma((16,)), dma, dma, dma, dma, dma((3,)), dma((3,)),
                 dma((3,)), dma((3,)), dma((4, 3)), dma((4, 3)), dma, dma, dma((4, 5)), dma((4, 5)),
             ],
             compiler_params=pltpu.CompilerParams(
-                collective_id=0, has_side_effects=True, vmem_limit_bytes=48 << 20
+                collective_id=0, has_side_effects=True, vmem_limit_bytes=67043328
             ),
         )(x, coord.reshape(1, width), level.reshape(1, width))
 

time: 79.1 us -> 61.6 us (0.78); the launches traced: 78 us -> 61.5 us
  Pallas kernels: 74.4 us -> 59.6 us
  local copies, waits for them, and re-layouts: 3.57 us -> 1.87 us
    pallas_call x1, Pallas kernels: 74.4 us -> 59.6 us  [per_device(): pl.pallas_call(body, out_shape=jax.ShapeDtypeStruct((owned, 4 * width), F...]
    unnamed x7 -> x1, local copies, waits for them, and re-layouts: 3.57 us -> 1.87 us
where the time goes in v2:
time: 61.6 us; the launch traced here: 61.5 us
  Pallas kernels  59.6 us (97%)
  local copies, waits for them, and re-layouts  1.87 us (3%)
    pallas_call x1, Pallas kernels, per_device(): pl.pallas_call(body, out_shape=jax.ShapeDtypeStruct((owned, 4 * width), F...  59.6 us
    unnamed x1, local copies, waits for them, and re-layouts  1.87 us

profile of v2, /device:TPU:1, one launch (start us, length us, event | category | flops | bytes accessed | tf_op | source)
XLA Modules:
  0.0 61.5 jit_solution(5264957775732417834)
XLA Ops:
  0.0 59.6 %shard_map.37 = f32[64,2048]{1,0:T(8,128)} custom-call(bf16[1536,512]{1,0:T(8,128)(2,1)} %x_ref.1, s32[1,512]{1,0:T(1,128)} %bitcast.2, s32[1,512]{1,0:T(1,128)} %bitcast.3), custom_call_target="tpu_custom_call" | custom-call | tf_op jit(solution)/shard_map/pallas_call | solution.py:320
  59.6 1.9 %copy.5 = f32[64,2048]{1,0:T(8,128)} copy(f32[64,2048]{1,0:T(8,128)} %shard_map.37) | data formatting | bytes 1048576

commit v3 on v2

--- a/solution.py
+++ b/solution.py
@@ -51,8 +51,8 @@
     members, parts, period, reach,
     x_ref, coord_hbm, level_hbm, out_ref,
     coord_ref, level_ref, held, turned, coords, rowv, weight, own_e, own_l, keep_e, keep_l, split,
-    ysend_e, yrecv_e, ysend_l, yrecv_l, fsend_e, frecv_e, fsend_l, frecv_l,
-    own_sem, note_sem, zs, zr, bs, br, us, ur, cs, cr, yse, yre, ysl, yrl, fse, fre, fsl, frl,
+    ysend_e, yrecv_e, ysend_m, yrecv_m, ysend_s, yrecv_s, fsend_e, frecv_e, fsend_l, frecv_l,
+    own_sem, note_sem, zs, zr, bs, br, us, ur, cs, cr, yse, yre, ysm, yrm, yss, yrs, fse, fre, fsl, frl,
 ):
     p, m = lax.axis_index("mesh"), lax.axis_index("mem")
     core, y, h = lax.rem(p, 2), m // 2, lax.rem(m, 2)
@@ -94,18 +94,12 @@
         c, r = pl.ds(i // 4 * LANES, LANES), pl.ds(i % 4 * piece, piece)
         return send(x_ref.at[r, c], held.at[2, r, c], zs.at[i], zr.at[i], (at(-2), m))
 
-    def pump(*counts):
-        for who, count in enumerate(counts):
-            if count:
-                todo = range(started[who], started[who] + count)
-                started[who] += count
-
-                @pl.when(core == who)
-                def _(todo=todo):
-                    for i in todo:
-                        if i >= 4:
-                            down(i - 4).wait_send()
-                        down(i).start()
+    def pump(who, count):
+        for i in range(started[who], started[who] + count):
+            if i >= 4:
+                down(i - 4).wait_send()
+            down(i).start()
+        started[who] += count
 
     beside = send(x_ref, held.at[1], bs, br, (sib, m))
     up = send(x_ref, held.at[3], us, ur, (at(1), m))
@@ -114,11 +108,14 @@
         note.start()
     beside.start()
 
+    @pl.when(core == 0)
+    def _():
+        pump(0, 4)
+
     @pl.when(core == 1)
     def _():
         up.start()
 
-    pump(4, 0)
     for copy in mine:
         copy.wait()
 
@@ -148,7 +145,13 @@
     for k, b in enumerate(e_blocks(y)):
         own_e[k] = b
 
-    pump(3, 3)
+    @pl.when(core == 0)
+    def _():
+        pump(0, 3)
+
+    @pl.when(core == 1)
+    def _():
+        pump(1, 3)
 
     def as_rows(ref):
         line = ref[0:1, columns(y)].astype(F32)
@@ -177,115 +180,211 @@
 
     beside.wait_recv()
     turn(1, 1)
-    pump(3, 3)
+    deep = parts // 4
+    z = lax.rem(p // 2, deep)
+    ends = jnp.logical_or(z == 0, z == deep - 1)
+    waiting = {0: [], 1: []}
+
+    def launch(who, *copies):
+        if waiting[who] is None:
+            for copy in copies:
+                copy.start()
+        else:
+            waiting[who] += copies
+
+            @pl.when(jnp.logical_not(ends))
+            def _():
+                for copy in copies:
+                    copy.start()
+
+    def flush(who):
+        @pl.when(ends)
+        def _():
+            for copy in waiting[who]:
+                copy.start()
+
+        waiting[who] = None
 
     f_e = send(fsend_e, frecv_e, fse, fre, (p, far))
-    for d in (1, 2, 3):
-        y_e(d).wait_recv()
-    scales = [scale_of(yrecv_e.at[d], 512) for d in range(3)]
-    theirs = []
-    for k in range(4):
-        total = own_e[k]
-        for d in range(3):
-            total = total + decode(yrecv_e.at[d], k * LANES, LANES, scales[d])
-        split[0, 0] = total[0:64]
-        split[0, 1] = total[64:128]
-        keep_e[k] = split[0, h]
-        theirs.append(split[0, 1 - h])
-
-    def put_e(a, n, v):
-        fsend_e[pl.ds(a, n), :] = v
-
-    encode(theirs, put_e)
-    f_e.start()
-    for _ in range(4):
-        pump(1, 1)
-
-    @pl.when(core == 0)
-    def _():
-        up.wait_recv()
-        turn(3, 2)
-
-    def third_e():
+
+    def e_second(who):
+        for d in (1, 2, 3):
+            y_e(d).wait_recv()
+        scales = [scale_of(yrecv_e.at[d], 512) for d in range(3)]
+        theirs = []
+        for k in range(4):
+            total = own_e[k]
+            for d in range(3):
+                total = total + decode(yrecv_e.at[d], k * LANES, LANES, scales[d])
+            split[0, 0] = total[0:64]
+            split[0, 1] = total[64:128]
+            keep_e[k] = split[0, h]
+            theirs.append(split[0, 1 - h])
+
+        def put(a, n, v):
+            fsend_e[pl.ds(a, n), :] = v
+
+        encode(theirs, put)
+        launch(who, f_e)
+
+    def e_third():
         f_e.wait_recv()
         scale = scale_of(frecv_e, 256)
         for k in range(4):
             finish(keep_e[k] + decode(frecv_e, k * 64, 64, scale), 0, k)
 
-    lhs2, rhs2 = 1 + (1 - core), 2 * (1 - core)
-
-    def l_blocks(row, j):
-        c = pl.ds(j * LANES, LANES)
+    def y_m(j, d):
+        return send(ysend_m.at[j, d - 1], yrecv_m.at[j, d - 1], ysm.at[j, d - 1], yrm.at[j, d - 1], ring(d))
+
+    def y_s(j, d):
+        return send(ysend_s.at[j, d - 1], yrecv_s.at[j, d - 1], yss.at[j, d - 1], yrs.at[j, d - 1], ring(d))
+
+    def m_blocks(row, j):
         pair = turned[row, 0:2].reshape(2 * LANES, members // 8)
-        both = jnp.dot(pair, held[2, :, c], preferred_element_type=F32)
-        third = jnp.dot(turned[row, lhs2], held[rhs2, :, c], preferred_element_type=F32)
-        return [both[0:LANES], both[LANES:], third]
-
-    def y_l(j, d):
-        return send(ysend_l.at[j, d - 1], yrecv_l.at[j, d - 1], ysl.at[j, d - 1], yrl.at[j, d - 1], ring(d))
-
-    def first(j):
+        both = jnp.dot(pair, held[2, :, pl.ds(j * LANES, LANES)], preferred_element_type=F32)
+        return [both[0:LANES], both[LANES:]]
+
+    def m_first(j):
         for i in range(4):
             down(4 * j + i).wait_recv()
         for d in (2, 1, 3):
 
             def put(a, n, v, d=d):
-                ysend_l[j, d - 1, pl.ds(a, n), :] = v
-
-            encode(l_blocks(lax.rem(y + d, 4), j), put)
-            y_l(j, d).start()
-        for k, b in enumerate(l_blocks(y, j)):
+                ysend_m[j, d - 1, pl.ds(a, n), :] = v
+
+            encode(m_blocks(lax.rem(y + d, 4), j), put)
+            y_m(j, d).start()
+        for k, b in enumerate(m_blocks(y, j)):
             own_l[j, k] = b
+
+    def s_first(j, left, right):
+        rhs = held.at[right, :, pl.ds(j * LANES, LANES)]
+        for d in (2, 1, 3):
+
+            def put(a, n, v, d=d):
+                ysend_s[j, d - 1, pl.ds(a, n), :] = v
+
+            encode([jnp.dot(turned[lax.rem(y + d, 4), left], rhs[...], preferred_element_type=F32)], put)
+            y_s(j, d).start()
+        own_l[j, 2] = jnp.dot(turned[y, left], rhs[...], preferred_element_type=F32)
 
     goals = [(p, far), (sib, m), (sib, far), (at(-1), m), (at(-1), far)]
 
     def f_l(j, i):
         return send(fsend_l.at[j, i], frecv_l.at[j, i], fsl.at[j, i], frl.at[j, i], goals[i])
 
-    def second(j):
+    def gathered(j, k, recv, at_row, scales):
+        total = own_l[j, k]
+        for d in range(3):
+            total = total + decode(recv.at[j, d], at_row, LANES, scales[d])
+        split[k, 0] = total[0:64]
+        split[k, 1] = total[64:128]
+
+    def forward(who, j, i, value):
+        def put(a, n, v):
+            fsend_l[j, i, pl.ds(a, n), :] = v
+
+        encode([value], put)
+        if i == 1:
+            f_l(j, i).start()
+        else:
+            launch(who, f_l(j, i))
+
+    def m_second(who, j):
         for d in (1, 2, 3):
-            y_l(j, d).wait_recv()
-        scales = [scale_of(yrecv_l.at[j, d], 384) for d in range(3)]
-        for k in range(3):
-            total = own_l[j, k]
-            for d in range(3):
-                total = total + decode(yrecv_l.at[j, d], k * LANES, LANES, scales[d])
-            split[k, 0] = total[0:64]
-            split[k, 1] = total[64:128]
+            y_m(j, d).wait_recv()
+        scales = [scale_of(yrecv_m.at[j, d], 256) for d in range(3)]
+        gathered(j, 0, yrecv_m, 0, scales)
+        forward(who, j, 0, split[0, 1 - h])
+        gathered(j, 1, yrecv_m, LANES, scales)
+        forward(who, j, 2, split[1, 1 - h])
+        forward(who, j, 1, split[1, h])
         keep_l[j] = split[0, h]
-        for i, (k, half) in enumerate([(0, 1 - h), (1, h), (1, 1 - h), (2, h), (2, 1 - h)]):
-
-            def put(a, n, v, i=i):
-                fsend_l[j, i, pl.ds(a, n), :] = v
-
-            encode([split[k, half]], put)
-            f_l(j, i).start()
-
-    def third(j):
-        for i in range(5):
-            f_l(j, i).wait_recv()
-        got = [decode(frecv_l.at[j, i], 0, 64, scale_of(frecv_l.at[j, i], 64)) for i in range(5)]
-        finish(keep_l[j] + got[0], 2, j)
-        finish(got[1] + got[2], 3 - 2 * core, j)
-        finish(got[3] + got[4], 1 + 2 * core, j)
-
-    first(0)
-    pump(1, 1)
-    first(1)
-    pump(1, 1)
-    second(0)
-    pump(0, 2)
-    pump(0, 2)
-    first(2)
-    second(1)
-    first(3)
-    third_e()
-    third(0)
-    second(2)
-    third(1)
-    second(3)
-    third(2)
-    third(3)
+
+    def s_second(who, j):
+        for d in (1, 2, 3):
+            y_s(j, d).wait_recv()
+        gathered(j, 2, yrecv_s, 0, [scale_of(yrecv_s.at[j, d], 128) for d in range(3)])
+        forward(who, j, 4, split[2, 1 - h])
+        forward(who, j, 3, split[2, h])
+
+    def got(j, i):
+        f_l(j, i).wait_recv()
+        return decode(frecv_l.at[j, i], 0, 64, scale_of(frecv_l.at[j, i], 64))
+
+    def third_a(j):
+        finish(keep_l[j] + got(j, 0), 2, j)
+
+    def third_b(j):
+        finish(got(j, 1) + got(j, 2), 3 - 2 * core, j)
+
+    def third_c(j):
+        finish(got(j, 3) + got(j, 4), 1 + 2 * core, j)
+
+    @pl.when(core == 0)
+    def _():
+        pump(0, 1)
+        m_first(0)
+        pump(0, 2)
+        e_second(0)
+        pump(0, 1)
+        m_first(1)
+        pump(0, 2)
+        m_second(0, 0)
+        pump(0, 1)
+        up.wait_recv()
+        turn(3, 2)
+        pump(0, 1)
+        s_first(0, 2, 2)
+        s_first(1, 2, 2)
+        pump(0, 1)
+        m_first(2)
+        m_second(0, 1)
+        s_first(2, 2, 2)
+        s_second(0, 0)
+        s_second(0, 1)
+        m_first(3)
+        s_first(3, 2, 2)
+        m_second(0, 2)
+        s_second(0, 2)
+        flush(0)
+        s_second(0, 3)
+        m_second(0, 3)
+
+    @pl.when(core == 1)
+    def _():
+        pump(1, 1)
+        s_first(0, 1, 0)
+        s_first(1, 1, 0)
+        pump(1, 2)
+        s_first(2, 1, 0)
+        s_first(3, 1, 0)
+        pump(1, 2)
+        e_second(1)
+        m_first(0)
+        pump(1, 1)
+        s_second(1, 0)
+        s_second(1, 1)
+        pump(1, 1)
+        s_second(1, 2)
+        s_second(1, 3)
+        pump(1, 2)
+        m_first(1)
+        pump(1, 1)
+        m_second(1, 0)
+        pump(1, 3)
+        m_first(2)
+        m_second(1, 1)
+        m_second(1, 2)
+        m_first(3)
+        flush(1)
+        m_second(1, 3)
+
+    e_third()
+    for j in range(4):
+        third_c(j)
+        third_a(j)
+        third_b(j)
     assert started == [16, 16]
 
     beside.wait_send()
@@ -303,7 +402,8 @@
         down(i).wait_send()
     for j in range(4):
         for d in (1, 2, 3):
-            y_l(j, d).wait_send()
+            y_m(j, d).wait_send()
+            y_s(j, d).wait_send()
         for i in range(5):
             f_l(j, i).wait_send()
 
@@ -337,14 +437,16 @@
                 vmem((3, 2, 64, LANES), F32),
                 vmem((3, 528, LANES), i16),
                 vmem((3, 528, LANES), i16),
-                vmem((4, 3, 400, LANES), i16),
-                vmem((4, 3, 400, LANES), i16),
+                vmem((4, 3, 272, LANES), i16),
+                vmem((4, 3, 272, LANES), i16),
+                vmem((4, 3, 144, LANES), i16),
+                vmem((4, 3, 144, LANES), i16),
                 vmem((272, LANES), i16),
                 vmem((272, LANES), i16),
                 vmem((4, 5, 80, LANES), i16),
                 vmem((4, 5, 80, LANES), i16),
                 dma, dma((2,)), dma((16,)), dma((16,)), dma, dma, dma, dma, dma((3,)), dma((3,)),
-                dma((3,)), dma((3,)), dma((4, 3)), dma((4, 3)), dma, dma, dma((4, 5)), dma((4, 5)),
+                dma((3,)), dma((3,)), dma((4, 3)), dma((4, 3)), dma((4, 3)), dma((4, 3)), dma, dma, dma((4, 5)), dma((4, 5)),
             ],
             compiler_params=pltpu.CompilerParams(
                 collective_id=0, has_side_effects=True, vmem_limit_bytes=67043328

time: 61.6 us -> 60.6 us (0.984)
  Pallas kernels: 59.6 us -> 58.6 us
    pallas_call x1, Pallas kernels: 59.6 us -> 58.6 us  [per_device(): pl.pallas_call(body, out_shape=jax.ShapeDtypeStruct((owned, 4 * width), F...]
where the time goes in v3:
time: 60.6 us; the launch traced here: 60.5 us
  Pallas kernels  58.6 us (97%)
  local copies, waits for them, and re-layouts  1.87 us (3%)
    pallas_call x1, Pallas kernels, per_device(): pl.pallas_call(body, out_shape=jax.ShapeDtypeStruct((owned, 4 * width), F...  58.6 us
    unnamed x1, local copies, waits for them, and re-layouts  1.87 us

profile of v3, /device:TPU:1, one launch (start us, length us, event | category | flops | bytes accessed | tf_op | source)
XLA Modules:
  0.0 60.5 jit_solution(14156976200794007560)
XLA Ops:
  0.0 58.6 %shard_map.37 = f32[64,2048]{1,0:T(8,128)} custom-call(bf16[1536,512]{1,0:T(8,128)(2,1)} %x_ref.1, s32[1,512]{1,0:T(1,128)} %bitcast.2, s32[1,512]{1,0:T(1,128)} %bitcast.3), custom_call_target="tpu_custom_call" | custom-call | tf_op jit(solution)/shard_map/pallas_call | solution.py:420
  58.6 1.9 %copy.5 = f32[64,2048]{1,0:T(8,128)} copy(f32[64,2048]{1,0:T(8,128)} %shard_map.37) | data formatting | bytes 1048576

commit v4 on v3

--- a/solution.py
+++ b/solution.py
@@ -50,7 +50,7 @@
 def kernel(
     members, parts, period, reach,
     x_ref, coord_hbm, level_hbm, out_ref,
-    coord_ref, level_ref, held, turned, coords, rowv, weight, own_e, own_l, keep_e, keep_l, split,
+    coord_ref, level_ref, held, turned, begun, coords, rowv, weight, own_e, own_l, keep_e, keep_l, split,
     ysend_e, yrecv_e, ysend_m, yrecv_m, ysend_s, yrecv_s, fsend_e, frecv_e, fsend_l, frecv_l,
     own_sem, note_sem, zs, zr, bs, br, us, ur, cs, cr, yse, yre, ysm, yrm, yss, yrs, fse, fre, fsl, frl,
 ):
@@ -180,34 +180,9 @@
 
     beside.wait_recv()
     turn(1, 1)
-    deep = parts // 4
-    z = lax.rem(p // 2, deep)
-    ends = jnp.logical_or(z == 0, z == deep - 1)
-    waiting = {0: [], 1: []}
-
-    def launch(who, *copies):
-        if waiting[who] is None:
-            for copy in copies:
-                copy.start()
-        else:
-            waiting[who] += copies
-
-            @pl.when(jnp.logical_not(ends))
-            def _():
-                for copy in copies:
-                    copy.start()
-
-    def flush(who):
-        @pl.when(ends)
-        def _():
-            for copy in waiting[who]:
-                copy.start()
-
-        waiting[who] = None
-
     f_e = send(fsend_e, frecv_e, fse, fre, (p, far))
 
-    def e_second(who):
+    def e_second():
         for d in (1, 2, 3):
             y_e(d).wait_recv()
         scales = [scale_of(yrecv_e.at[d], 512) for d in range(3)]
@@ -225,7 +200,7 @@
             fsend_e[pl.ds(a, n), :] = v
 
         encode(theirs, put)
-        launch(who, f_e)
+        f_e.start()
 
     def e_third():
         f_e.wait_recv()
@@ -239,22 +214,37 @@
     def y_s(j, d):
         return send(ysend_s.at[j, d - 1], yrecv_s.at[j, d - 1], yss.at[j, d - 1], yrs.at[j, d - 1], ring(d))
 
-    def m_blocks(row, j):
-        pair = turned[row, 0:2].reshape(2 * LANES, members // 8)
-        both = jnp.dot(pair, held[2, :, pl.ds(j * LANES, LANES)], preferred_element_type=F32)
+    depth = members // 8
+    head = depth * 2 // 3
+
+    def m_product(row, j, start, size):
+        k = pl.ds(start, size)
+        pair = turned[row, 0:2, :, k].reshape(2 * LANES, size)
+        return jnp.dot(pair, held[2, k, pl.ds(j * LANES, LANES)], preferred_element_type=F32)
+
+    def m_blocks(d, j):
+        row = lax.rem(y + d, 4)
+        if j < 3:
+            both = m_product(row, j, 0, depth)
+        else:
+            both = begun[d] + m_product(row, j, head, depth - head)
         return [both[0:LANES], both[LANES:]]
 
     def m_first(j):
-        for i in range(4):
+        for i in range(3):
             down(4 * j + i).wait_recv()
+        if j == 3:
+            for d in range(4):
+                begun[d] = m_product(lax.rem(y + d, 4), j, 0, head)
+        down(4 * j + 3).wait_recv()
         for d in (2, 1, 3):
 
             def put(a, n, v, d=d):
                 ysend_m[j, d - 1, pl.ds(a, n), :] = v
 
-            encode(m_blocks(lax.rem(y + d, 4), j), put)
+            encode(m_blocks(d, j), put)
             y_m(j, d).start()
-        for k, b in enumerate(m_blocks(y, j)):
+        for k, b in enumerate(m_blocks(0, j)):
             own_l[j, k] = b
 
     def s_first(j, left, right):
@@ -280,33 +270,30 @@
         split[k, 0] = total[0:64]
         split[k, 1] = total[64:128]
 
-    def forward(who, j, i, value):
+    def forward(j, i, value):
         def put(a, n, v):
             fsend_l[j, i, pl.ds(a, n), :] = v
 
         encode([value], put)
-        if i == 1:
-            f_l(j, i).start()
-        else:
-            launch(who, f_l(j, i))
-
-    def m_second(who, j):
+        f_l(j, i).start()
+
+    def m_second(j):
         for d in (1, 2, 3):
             y_m(j, d).wait_recv()
         scales = [scale_of(yrecv_m.at[j, d], 256) for d in range(3)]
         gathered(j, 0, yrecv_m, 0, scales)
-        forward(who, j, 0, split[0, 1 - h])
+        forward(j, 0, split[0, 1 - h])
         gathered(j, 1, yrecv_m, LANES, scales)
-        forward(who, j, 2, split[1, 1 - h])
-        forward(who, j, 1, split[1, h])
+        forward(j, 2, split[1, 1 - h])
+        forward(j, 1, split[1, h])
         keep_l[j] = split[0, h]
 
-    def s_second(who, j):
+    def s_second(j):
         for d in (1, 2, 3):
             y_s(j, d).wait_recv()
         gathered(j, 2, yrecv_s, 0, [scale_of(yrecv_s.at[j, d], 128) for d in range(3)])
-        forward(who, j, 4, split[2, 1 - h])
-        forward(who, j, 3, split[2, h])
+        forward(j, 4, split[2, 1 - h])
+        forward(j, 3, split[2, h])
 
     def got(j, i):
         f_l(j, i).wait_recv()
@@ -326,11 +313,11 @@
         pump(0, 1)
         m_first(0)
         pump(0, 2)
-        e_second(0)
+        e_second()
         pump(0, 1)
         m_first(1)
         pump(0, 2)
-        m_second(0, 0)
+        m_second(0)
         pump(0, 1)
         up.wait_recv()
         turn(3, 2)
@@ -339,17 +326,22 @@
         s_first(1, 2, 2)
         pump(0, 1)
         m_first(2)
-        m_second(0, 1)
+        m_second(1)
         s_first(2, 2, 2)
-        s_second(0, 0)
-        s_second(0, 1)
+        s_second(0)
+        s_second(1)
         m_first(3)
         s_first(3, 2, 2)
-        m_second(0, 2)
-        s_second(0, 2)
-        flush(0)
-        s_second(0, 3)
-        m_second(0, 3)
+        m_second(2)
+        s_second(2)
+        e_third()
+        for j in range(2):
+            third_a(j)
+            third_b(j)
+        for j in range(4):
+            third_c(j)
+        s_second(3)
+        m_second(3)
 
     @pl.when(core == 1)
     def _():
@@ -360,29 +352,32 @@
         s_first(2, 1, 0)
         s_first(3, 1, 0)
         pump(1, 2)
-        e_second(1)
+        e_second()
         m_first(0)
         pump(1, 1)
-        s_second(1, 0)
-        s_second(1, 1)
+        s_second(0)
+        s_second(1)
         pump(1, 1)
-        s_second(1, 2)
-        s_second(1, 3)
+        s_second(2)
+        s_second(3)
         pump(1, 2)
         m_first(1)
         pump(1, 1)
-        m_second(1, 0)
+        m_second(0)
         pump(1, 3)
         m_first(2)
-        m_second(1, 1)
-        m_second(1, 2)
+        m_second(1)
+        e_third()
+        for j in range(2):
+            third_a(j)
+            third_b(j)
+        m_second(2)
         m_first(3)
-        flush(1)
-        m_second(1, 3)
-
-    e_third()
-    for j in range(4):
-        third_c(j)
+        m_second(3)
+        for j in range(4):
+            third_c(j)
+
+    for j in (2, 3):
         third_a(j)
         third_b(j)
     assert started == [16, 16]
@@ -427,6 +422,7 @@
                 vmem((1, width), jnp.int32),
                 vmem((4, rows, width), jnp.bfloat16),
                 vmem((4, 3, LANES, rows), jnp.bfloat16),
+                vmem((4, 2 * LANES, LANES), F32),
                 vmem((3, 1, width), jnp.int32),
                 vmem((2, 2, 64, LANES), F32),
                 vmem((4, 4, 64, LANES), F32),

time: 60.6 us -> 60.5 us (level)
  no operation moved by 1% of the time
where the time goes in v4:
time: 60.5 us; the launch traced here: 60.4 us
  Pallas kernels  58.5 us (97%)
  local copies, waits for them, and re-layouts  1.87 us (3%)
    pallas_call x1, Pallas kernels, per_device(): pl.pallas_call(body, out_shape=jax.ShapeDtypeStruct((owned, 4 * width), F...  58.5 us
    unnamed x1, local copies, waits for them, and re-layouts  1.87 us

profile of v4, /device:TPU:1, one launch (start us, length us, event | category | flops | bytes accessed | tf_op | source)
XLA Modules:
  0.0 60.4 jit_solution(4329593022009726012)
XLA Ops:
  0.0 58.5 %shard_map.37 = f32[64,2048]{1,0:T(8,128)} custom-call(bf16[1536,512]{1,0:T(8,128)(2,1)} %x_ref.1, s32[1,512]{1,0:T(1,128)} %bitcast.2, s32[1,512]{1,0:T(1,128)} %bitcast.3), custom_call_target="tpu_custom_call" | custom-call | tf_op jit(solution)/shard_map/pallas_call | solution.py:415
  58.5 1.9 %copy.5 = f32[64,2048]{1,0:T(8,128)} copy(f32[64,2048]{1,0:T(8,128)} %shard_map.37) | data formatting | bytes 1048576

commit v5 on v4

--- a/solution.py
+++ b/solution.py
@@ -115,6 +115,7 @@
     @pl.when(core == 1)
     def _():
         up.start()
+        pump(1, 3)
 
     for copy in mine:
         copy.wait()
@@ -151,7 +152,7 @@
 
     @pl.when(core == 1)
     def _():
-        pump(1, 3)
+        pump(1, 1)
 
     def as_rows(ref):
         line = ref[0:1, columns(y)].astype(F32)
@@ -364,7 +365,7 @@
         m_first(1)
         pump(1, 1)
         m_second(0)
-        pump(1, 3)
+        pump(1, 2)
         m_first(2)
         m_second(1)
         e_third()

time: 60.5 us -> 59.1 us (0.977)
  Pallas kernels: 58.5 us -> 56.8 us
    pallas_call x1, Pallas kernels: 58.5 us -> 56.8 us  [per_device(): pl.pallas_call(body, out_shape=jax.ShapeDtypeStruct((owned, 4 * width), F...]
where the time goes in v5:
time: 59.1 us; the launch traced here: 58.7 us
  Pallas kernels  56.8 us (96%)
  local copies, waits for them, and re-layouts  1.87 us (3%)
    pallas_call x1, Pallas kernels, per_device(): pl.pallas_call(body, out_shape=jax.ShapeDtypeStruct((owned, 4 * width), F...  56.8 us
    unnamed x1, local copies, waits for them, and re-layouts  1.87 us

profile of v5, /device:TPU:1, one launch (start us, length us, event | category | flops | bytes accessed | tf_op | source)
XLA Modules:
  0.0 58.7 jit_solution(11281315959365048324)
XLA Ops:
  0.0 56.8 %shard_map.37 = f32[64,2048]{1,0:T(8,128)} custom-call(bf16[1536,512]{1,0:T(8,128)(2,1)} %x_ref.1, s32[1,512]{1,0:T(1,128)} %bitcast.2, s32[1,512]{1,0:T(1,128)} %bitcast.3), custom_call_target="tpu_custom_call" | custom-call | tf_op jit(solution)/shard_map/pallas_call | solution.py:416
  56.8 1.9 %copy.5 = f32[64,2048]{1,0:T(8,128)} copy(f32[64,2048]{1,0:T(8,128)} %shard_map.37) | data formatting | bytes 1048576

commit v6 on v5

--- a/solution.py
+++ b/solution.py
@@ -114,8 +114,8 @@
 
     @pl.when(core == 1)
     def _():
+        pump(1, 4)
         up.start()
-        pump(1, 3)
 
     for copy in mine:
         copy.wait()
@@ -149,10 +149,6 @@
     @pl.when(core == 0)
     def _():
         pump(0, 3)
-
-    @pl.when(core == 1)
-    def _():
-        pump(1, 1)
 
     def as_rows(ref):
         line = ref[0:1, columns(y)].astype(F32)

time: 59.1 us -> 59.1 us (level)
  no operation moved by 1% of the time
where the time goes in v6:
time: 59.1 us; the launch traced here: 58.7 us
  Pallas kernels  56.8 us (96%)
  local copies, waits for them, and re-layouts  1.87 us (3%)
    pallas_call x1, Pallas kernels, per_device(): pl.pallas_call(body, out_shape=jax.ShapeDtypeStruct((owned, 4 * width), F...  56.8 us
    unnamed x1, local copies, waits for them, and re-layouts  1.87 us

profile of v6, /device:TPU:1, one launch (start us, length us, event | category | flops | bytes accessed | tf_op | source)
XLA Modules:
  0.0 58.7 jit_solution(4918557389902185453)
XLA Ops:
  0.0 56.8 %shard_map.37 = f32[64,2048]{1,0:T(8,128)} custom-call(bf16[1536,512]{1,0:T(8,128)(2,1)} %x_ref.1, s32[1,512]{1,0:T(1,128)} %bitcast.2, s32[1,512]{1,0:T(1,128)} %bitcast.3), custom_call_target="tpu_custom_call" | custom-call | tf_op jit(solution)/shard_map/pallas_call | solution.py:412
  56.8 1.9 %copy.5 = f32[64,2048]{1,0:T(8,128)} copy(f32[64,2048]{1,0:T(8,128)} %shard_map.37) | data formatting | bytes 1048576
